TPU v7x, 32 devices: a whole 2x2x4 slice. The times are simulated.
32 devices in a mesh: groups: 2 (over x), corpus: 16 (over z, y, core).
Axes of the slice: x: 2, y: 2, z: 4, core: 2. Of those that a mesh axis runs over, the one named last changes fastest.
Arguments:
- queries: bfloat16 [1792, 32, 128], P(('groups', 'corpus')), parts along dimension 0, may hold values from -6 to 6
- passages: bfloat16 [4096, 128, 128], P(('groups', 'corpus')), parts along dimension 0, may hold values from -0.5 to 0.5
- lengths: int32 [4096], P(('groups', 'corpus')), parts along dimension 0, may hold values from 8 to 128
- candidates: int32 [32, 128], P(('groups', 'corpus')), parts along dimension 0, may hold values from 0 to 2047, as said below
Outputs:
- scores: float32 [1792, 128], P(('groups', 'corpus')), parts along dimension 0
- best_scores: float32 [1792, 100], P(('groups', 'corpus')), parts along dimension 0
There are 2 independent parts, one for each index of `groups`. A program takes and returns all parts, laid end to end along the dimension named above; each array names one. Nothing has to cross between parts.
Inputs may be any that keep to these rules, and one draw needn't show every extreme that they name: Row b lists the candidates of queries b * 56 to (b + 1) * 56 - 1. Passage p is held by owner p // 128. In every row at most 12 entries share an owner, and in every row some owner holds exactly 12 of them. Entries may repeat. `lengths`: rows of a tile at or past its length are padding.
All inputs are finite; a program needn't handle non-finite values.
Results may differ from a plain program's by a relative error of at most 0.0003.
Values may be sent and summed in bfloat16 or wider, within the bound.
A program may use at most 128 MiB of HBM per device.

v0:
```python
import math

import jax
import jax.numpy as jnp
from jax import lax
from jax.sharding import PartitionSpec as P

TOPK = 100


def maxsim_many(query_sets, tile_sets, per_device):
    similar = jnp.einsum(
        "srd,sgpd->srgp", query_sets, tile_sets, preferred_element_type=jnp.float32
    )
    nearest = jnp.max(similar, axis=3)
    shards_now = query_sets.shape[0]
    query_tok = query_sets.shape[1] // per_device
    return jnp.sum(
        nearest.reshape(shards_now, per_device, query_tok, nearest.shape[2]), axis=2
    ) / float(query_tok)


def fill_rows(tile_set, tile_len):
    inside = lax.broadcasted_iota(jnp.int32, tile_set.shape[:2], 1) < tile_len[:, None]
    return jnp.where(inside[:, :, None], tile_set, tile_set[:, :1, :])


def local(queries, passages, lengths, candidates):
    peers = lax.axis_size("corpus")
    per_owner, tile_rows, feature = passages.shape
    per_device, query_tok = (queries.shape[0], queries.shape[1])
    candidate_ids = candidates[0]
    number = candidate_ids.shape[0]
    capacity = max(2, 3 * number // (2 * peers))
    owner_of = candidate_ids // per_owner
    local_id = candidate_ids - owner_of * per_owner
    position = jnp.arange(number, dtype=jnp.int32)
    shared = (owner_of[:, None] == owner_of[None, :]) & (position[None, :] < position[:, None])
    rank_in = jnp.sum(shared.astype(jnp.int32), axis=1)
    slot_of = owner_of * capacity + rank_in
    matches = slot_of[None, :] == jnp.arange(peers * capacity, dtype=jnp.int32)[:, None]
    wanted = jnp.max(jnp.where(matches, local_id[None, :], -1), axis=1).reshape(peers, capacity)
    asked = lax.all_to_all(wanted, "corpus", split_axis=0, concat_axis=0, tiled=True)
    picked = jnp.maximum(asked.reshape(-1), 0)
    chosen = fill_rows(passages[picked], lengths[picked])
    by_scorer = chosen.reshape(peers, capacity, tile_rows, feature)
    stacked = queries.reshape(1, per_device * query_tok, feature)
    piece = lax.all_gather(stacked, "corpus", axis=0, tiled=True)
    shards_here = piece.shape[0]
    group_size = math.gcd(shards_here, 8)
    turns = shards_here // group_size
    query_groups = piece.reshape(turns, group_size, piece.shape[1], feature)
    tile_groups = by_scorer.reshape(turns, group_size, capacity, tile_rows, feature)
    fresh_scores = lax.map(
        lambda paired: maxsim_many(paired[0], paired[1], per_device), (query_groups, tile_groups)
    )
    fresh_scores = fresh_scores.reshape(shards_here, per_device, capacity)
    returned = lax.all_to_all(fresh_scores, "corpus", split_axis=0, concat_axis=0, tiled=True)
    spread = jnp.transpose(returned, (1, 0, 2)).reshape(per_device, peers * capacity)
    scores = jnp.take(spread, slot_of, axis=1)
    best_scores = lax.top_k(scores, TOPK)[0]
    return (scores, best_scores)


def solution(mesh):
    return jax.shard_map(
        local,
        mesh=mesh,
        in_specs=(
            P(("groups", "corpus"), None, None),
            P(("groups", "corpus"), None, None),
            P(("groups", "corpus")),
            P(("groups", "corpus"), None),
        ),
        out_specs=(P(("groups", "corpus"), None), P(("groups", "corpus"), None)),
        check_vma=False,
    )
```

profile of v0, /device:TPU:0, one launch (start us, length us, event | category | flops | bytes accessed | tf_op | source)
XLA Modules:
  0.0 137.0 jit_solution(5977993929277204286)
XLA Ops:
  7.2 0.7 all-gather.2.cloned.1.call-update
  7.9 0.7 subtract_bitcast_fusion
  8.6 0.7 and_select_fusion.2
  9.2 0.2 convert_reduce_fusion
  9.4 0.1 select_reduce_fusion
  9.6 0.7 all_to_all.9
  10.3 7.4 %all-to-all-start = ((s32[16,1,12]{2,1,0:T(1,128)}), s32[16,1,12]{2,1,0:T(1,128)S(1)}, u32[]{:S(2)}, u32[]{:S(2)}) async-start(s32[16,1,12]{2,1,0:T(1,128)} %bitcast.12), calls=%async_computation | async-start | bytes 16384 | tf_op jit(solution)/shard_map/all_to_all | solution.py:43
  17.7 0.7 fusion.6
  18.3 0.7 compare_and_fusion
  19.0 5.0 %all-to-all-done = s32[16,1,12]{2,1,0:T(1,128)S(1)} async-done(((s32[16,1,12]{2,1,0:T(1,128)}), s32[16,1,12]{2,1,0:T(1,128)S(1)}, u32[]{:S(2)}, u32[]{:S(2)}) %all-to-all-start) | async-done | bytes 800 | tf_op jit(solution)/shard_map/all_to_all | solution.py:43
  24.2 10.2 %gather_fusion.1 = bf16[192,128,128]{2,1,0:T(8,128)(2,1)} fusion(bf16[128,128,128]{2,1,0:T(8,128)(2,1)} %param.7, s32[1024]{0:T(1024)S(1)} %pad_clamp_fusion.1), kind=kCustom, calls=%fused_computation.1 | custom fusion | bytes 12583680 | tf_op jit(solution)/shard_map/gather | solution.py:45
  34.3 1.3 slice_reduce_fusion
  35.6 1.6 %gather_fusion = s32[192]{0:T(256)S(1)} fusion(s32[128]{0:T(128)S(1)} %copy-done, s32[1024]{0:T(1024)S(1)} %pad_clamp_fusion.1), kind=kCustom, calls=%fused_computation | custom fusion | bytes 2304 | tf_op jit(solution)/shard_map/gather | solution.py:45
  37.3 0.1 iota_compare_fusion
  37.4 6.5 %broadcast_select_fusion = bf16[2,8,12,128,128]{4,3,2,1,0:T(8,128)(2,1)} fusion(bf16[2,8,12,128,128]{4,3,2,1,0:T(8,128)(2,1)} %bitcast.73, pred[2,8,12,128]{3,2,1,0:T(8,128)(4,1)S(1)} %iota_compare_fusion, bf16[2,8,12,128]{3,2,1,0:T(8,128)(2,1)S(1)} %broadcast_in_dim.64), kind=kLoop, calls=%fused_computation.10 | loop fusion | flops 3145728 | bytes 12656640 | tf_op jit(solution)/shard_map/jit(_where)/select_n | solution.py:25
  43.9 36.8 %all-gather.2.cloned.1.call-done = bf16[16,1792,128]{2,1,0:T(8,128)(2,1)} async-done(((bf16[1,1792,128]{2,1,0:T(8,128)(2,1)}), bf16[16,1792,128]{2,1,0:T(8,128)(2,1)}) %all-gather.2.cloned.1.call-update) | async-done | bytes 7340048 | tf_op jit(solution)/shard_map/all_gather | solution.py:48
  80.7 32.9 %while.10 = (s32[]{:T(128)}, f32[2,8,56,12]{2,1,0,3:T(8,128)S(1)}, bf16[2,8,1792,128]{3,2,1,0:T(8,128)(2,1)}, bf16[2,8,12,128,128]{4,3,2,1,0:T(8,128)(2,1)}, s32[]{:T(128)}, /*index=5*/f32[]{:T(128)}) while((s32[]{:T(128)}, f32[2,8,56,12]{2,1,0,3:T(8,128)S(1)}, bf16[2,8,1792,128]{3,2,1,0:T(8,128)(2,1)}, ...), condition=%wide.region_5.6_spmd, body=%wide.region_2.5_spmd.sunk | while | flops 5659164672 | bytes 11065421 | solution.py:54
  80.7 14.4 %convolution_reduce_fusion.2 = f32[8,1792,12]{1,2,0:T(8,128)S(1)} fusion(bf16[2,8,1792,128]{3,2,1,0:T(8,128)(2,1)} %get-tuple-element.87, s32[]{:T(128)} %get-tuple-element.79, bf16[2,8,12,128,128]{4,3,2,1,0:T(8,128)(2,1)} %get-tuple-element.88), kind=kOutput, calls=%fused_computation.3.clone.1 | convolution fusion | flops 5658992640 | bytes 7504896 | tf_op jit(solution)/shard_map/while/body/eval_jaxpr/srd,sgpd->srgp/dot_general | solution.py:12
  95.1 0.4 copy.35
  95.5 0.8 reshape.220
  96.4 0.8 reduce_sum.27
  97.2 14.4 %convolution_reduce_fusion.2 = f32[8,1792,12]{1,2,0:T(8,128)S(1)} fusion(bf16[2,8,1792,128]{3,2,1,0:T(8,128)(2,1)} %get-tuple-element.87, s32[]{:T(128)} %get-tuple-element.79, bf16[2,8,12,128,128]{4,3,2,1,0:T(8,128)(2,1)} %get-tuple-element.88), kind=kOutput, calls=%fused_computation.3.clone.1 | convolution fusion | flops 5658992640 | bytes 7504896 | tf_op jit(solution)/shard_map/while/body/eval_jaxpr/srd,sgpd->srgp/dot_general | solution.py:12
  111.6 0.4 copy.35
  112.0 0.8 reshape.220
  112.8 0.8 reduce_sum.27
  113.7 0.8 reshape.217
  114.5 3.5 %all-to-all-start.1 = ((f32[16,1,672]{2,1,0:T(1,128)}), f32[16,1,672]{2,1,0:T(1,128)S(1)}, u32[]{:S(2)}, u32[]{:S(2)}) async-start(f32[16,1,672]{2,1,0:T(1,128)} %reshape.217), calls=%async_computation.1 | async-start | bytes 98304 | tf_op jit(solution)/shard_map/all_to_all | solution.py:58
  118.0 6.7 %all-to-all-done.1 = f32[16,1,672]{2,1,0:T(1,128)S(1)} async-done(((f32[16,1,672]{2,1,0:T(1,128)}), f32[16,1,672]{2,1,0:T(1,128)S(1)}, u32[]{:S(2)}, u32[]{:S(2)}) %all-to-all-start.1) | async-done | bytes 43040 | tf_op jit(solution)/shard_map/all_to_all | solution.py:58
  124.7 0.5 broadcast.219
  125.2 0.8 reduce.6
  126.1 0.6 gather_fusion.2
  126.9 3.2 %top_k.9 = (f32[56,128]{1,0:T(8,128)}, s32[56,128]{1,0:T(8,128)}) sort(f32[56,128]{1,0:T(8,128)S(1)} %copy.27, s32[56,128]{1,0:T(8,128)S(1)} %iota.22), dimensions={1}, to_apply=%region_6.7 | sort | flops 93184 | bytes 114688 | tf_op jit(solution)/shard_map/top_k | solution.py:61
  (22 shorter events, 0.6 us)
Async XLA Ops:
  7.2 28.5 %copy-start = (s32[128]{0:T(128)S(1)}, s32[128]{0:T(128)}, u32[]{:S(2)}) copy-start(s32[128]{0:T(128)} %param.8) | copy-start | bytes 1540
  7.2 73.5 %all-gather.2.cloned.1.call-start = ((), (), s32[]{:S(2)}) async-start(), calls=%async_computation.2 | async-start | bytes 7798784 | tf_op jit(solution)/shard_map/all_gather | solution.py:48
  10.3 13.8 %all-to-all-start = ((s32[16,1,12]{2,1,0:T(1,128)}), s32[16,1,12]{2,1,0:T(1,128)S(1)}, u32[]{:S(2)}, u32[]{:S(2)}) async-start(s32[16,1,12]{2,1,0:T(1,128)} %bitcast.12), calls=%async_computation | async-start | bytes 16384 | tf_op jit(solution)/shard_map/all_to_all | solution.py:43
  114.5 10.2 %all-to-all-start.1 = ((f32[16,1,672]{2,1,0:T(1,128)}), f32[16,1,672]{2,1,0:T(1,128)S(1)}, u32[]{:S(2)}, u32[]{:S(2)}) async-start(f32[16,1,672]{2,1,0:T(1,128)} %reshape.217), calls=%async_computation.1 | async-start | bytes 98304 | tf_op jit(solution)/shard_map/all_to_all | solution.py:58
  126.9 3.2 %copy-start.1 = (f32[56,128]{1,0:T(8,128)}, f32[56,128]{1,0:T(8,128)S(1)}, u32[]{:S(2)}) copy-start(f32[56,128]{1,0:T(8,128)S(1)} %copy.27) | copy-start | bytes 86020
Sparse Core Ops, SparseCore 0:
  10.3 70.3 all-gather.1
where the time goes:
time: 137 us
  waiting for transfers between devices  49.2 us (36%)
  matrix products  28.8 us (21%)
  local copies, waits for them, and re-layouts  18.4 us (13%)
  other arithmetic  15.3 us (11%)
  between operations  14.2 us (10%)
  starting transfers between devices  10.9 us (8%)
    all_gather x1, waiting for transfers between devices, local(): piece = lax.all_gather(stacked, 'corpus', axis=0, tiled=True)  36.8 us
    dot_general x2, matrix products, maxsim_many(): jnp.einsum('srd,sgpd->srgp', query_sets, tile_sets, preferred_element_typ...  28.8 us
    gather x2, local copies, waits for them, and re-layouts, local(): chosen = fill_rows(passages[picked], lengths[picked])  11.7 us
    all_to_all x1, starting transfers between devices, local(): lax.all_to_all(wanted, 'corpus', split_axis=0, concat_axis=0, tiled=True)  7.41 us
    all_to_all x1, waiting for transfers between devices, local(): lax.all_to_all(fresh_scores, 'corpus', split_axis=0, concat_axis=0, tiled...  6.72 us
    select_n x1, other arithmetic, fill_rows(): return jnp.where(inside[:, :, None], tile_set, tile_set[:, :1, :])  6.55 us
    all_to_all x1, waiting for transfers between devices, local(): lax.all_to_all(wanted, 'corpus', split_axis=0, concat_axis=0, tiled=True)  5.01 us
    all_to_all x1, starting transfers between devices, local(): lax.all_to_all(fresh_scores, 'corpus', split_axis=0, concat_axis=0, tiled...  3.5 us
  transfers between devices with their start and end apart: 3, of which 3 were waited for; matrix products, arithmetic and copies ran while one was open for 17% of the time, Pallas kernels for 0%

commit v1 on v0

v1 whole, which is shorter than its diff:
```python
import functools

import jax
import jax.numpy as jnp
from jax import lax
from jax.experimental import pallas as pl
from jax.experimental.pallas import tpu as pltpu
from jax.sharding import PartitionSpec as P

TOPK = 100
MESH = pl.DeviceIdType.MESH


def pick_tile(rows, tok):
    tile = 256
    while rows % tile or tile % tok:
        tile //= 2
    return tile


def kernel(cfg, cand_ref, len_ref, q_hbm, p_hbm, out_ref, qall, pas, cand_all,
           wanted_v, wanted_s, tiles, fold, send_buf, got, q_send, q_recv,
           sib_send, sib_recv, id_send, id_recv, sc_send, sc_recv, loc_sem):
    n, ways, cap, per_owner, tile_rows, rows, feature, tok, col = cfg
    chips = n // 2
    half = chips // 2
    depth = chips // ways
    units = rows // col
    cut = (units + 1) // 2
    spans = ((0, cut), (cut, units))
    me = lax.axis_index("corpus")
    core = lax.rem(me, 2)
    chip = me // 2
    if ways == 2:
        zz, yy = chip // 2, lax.rem(chip, 2)
        pos = (1 - yy) * zz + yy * (2 * depth - 1 - zz)
    else:
        pos = chip

    def at(p, c):
        p = lax.rem(p + 2 * chips, chips)
        if ways == 2:
            far = p // depth
            p = (1 - far) * (2 * p) + far * ((2 * depth - 1 - p) * 2 + 1)
        return p * 2 + c

    sib = at(pos, 1 - core)
    right, left = at(pos + 1, core), at(pos - 1, core)
    toward = (right, left)

    def origin(d, s, c):
        return at(pos - s if d == 0 else pos + s, c)

    def piece(b, k):
        lo, hi = spans[k]
        return qall.at[b, pl.ds(lo * col, (hi - lo) * col), :]

    def hop(d, s, k):
        b = origin(d, s - 1, core)
        return pltpu.make_async_remote_copy(
            src_ref=piece(b, k), dst_ref=piece(b, k),
            send_sem=q_send.at[d, s, k], recv_sem=q_recv.at[d, s, k],
            device_id={"corpus": toward[d]}, device_id_type=MESH)

    def hop_in(d, s, k):
        b = origin(d, s, core)
        return pltpu.make_async_remote_copy(
            src_ref=piece(b, k), dst_ref=piece(b, k),
            send_sem=q_send.at[d, s, k], recv_sem=q_recv.at[d, s, k],
            device_id={"corpus": toward[d]}, device_id_type=MESH)

    def share(d, s, k, c):
        b = origin(d, s, c)
        return pltpu.make_async_remote_copy(
            src_ref=piece(b, k), dst_ref=piece(b, k),
            send_sem=sib_send.at[d, s, k], recv_sem=sib_recv.at[d, s, k],
            device_id={"corpus": sib}, device_id_type=MESH)

    def has_hop(d, s, k):
        return 1 <= s < half or (s == half and k == d)

    def id_copy(o):
        peer = lax.rem(me + o, n)
        return pltpu.make_async_remote_copy(
            src_ref=cand_all.at[me], dst_ref=cand_all.at[me],
            send_sem=id_send.at[o], recv_sem=id_recv.at[me],
            device_id={"corpus": peer}, device_id_type=MESH)

    def id_in(o):
        peer = lax.rem(me + o, n)
        return pltpu.make_async_remote_copy(
            src_ref=cand_all.at[peer], dst_ref=cand_all.at[peer],
            send_sem=id_send.at[o], recv_sem=id_recv.at[peer],
            device_id={"corpus": peer}, device_id_type=MESH)

    def score_copy(b):
        return pltpu.make_async_remote_copy(
            src_ref=send_buf.at[b], dst_ref=got.at[me],
            send_sem=sc_send.at[b], recv_sem=sc_recv.at[me],
            device_id={"corpus": b}, device_id_type=MESH)

    def score_in(o):
        peer = lax.rem(me + o, n)
        return pltpu.make_async_remote_copy(
            src_ref=send_buf.at[peer], dst_ref=got.at[peer],
            send_sem=sc_send.at[peer], recv_sem=sc_recv.at[peer],
            device_id={"corpus": peer}, device_id_type=MESH)

    q_load = pltpu.make_async_copy(q_hbm, qall.at[me], loc_sem.at[0])
    c_load = pltpu.make_async_copy(cand_ref, cand_all.at[me], loc_sem.at[2])
    p_load = pltpu.make_async_copy(p_hbm, pas, loc_sem.at[1])
    c_load.start()
    q_load.start()
    p_load.start()

    barrier = pltpu.get_barrier_semaphore()

    def greet(o, _):
        pl.semaphore_signal(barrier, inc=1, device_id={"corpus": lax.rem(me + o, n)},
                            device_id_type=MESH)
        return 0

    lax.fori_loop(1, n, greet, 0)
    row_at = lax.broadcasted_iota(jnp.int32, (rows, 128), 0) // tok
    lane_at = lax.broadcasted_iota(jnp.int32, (rows, 128), 1)
    fold[...] = jnp.where(row_at == lane_at, 1.0, 0.0).astype(fold.dtype)
    c_load.wait()
    q_load.wait()
    pl.semaphore_wait(barrier, n - 1)

    def each(first, fn):
        def body(o, _):
            fn(o)
            return 0
        lax.fori_loop(first, n, body, 0)

    each(1, lambda o: id_copy(o).start())
    for k in range(2):
        for d in range(2):
            if has_hop(d, 1, k):
                hop(d, 1, k).start()
        share(0, 0, k, core).start()
    each(1, lambda o: id_in(o).wait_recv())

    ids = cand_all[...].reshape(n, cand_all.shape[2])
    number = ids.shape[1]
    owner = lax.div(ids, per_owner)
    local = ids - owner * per_owner
    mine = owner == me
    r_at = lax.broadcasted_iota(jnp.int32, (number, number), 0)
    c_at = lax.broadcasted_iota(jnp.int32, (number, number), 1)
    before = jnp.where(r_at < c_at, 1.0, 0.0).astype(jnp.bfloat16)
    rank = jnp.dot(jnp.where(mine, 1.0, 0.0).astype(jnp.bfloat16), before,
                   preferred_element_type=jnp.float32)
    lane = lax.broadcasted_iota(jnp.int32, (n, number), 1)
    wanted = jnp.zeros((n, number), jnp.int32)
    for s in range(cap):
        hit = mine & (rank == float(s))
        found = jnp.max(jnp.where(hit, local, 0), axis=1, keepdims=True)
        wanted = jnp.where(lane == s, found, wanted)
    wanted_v[...] = wanted
    w_load = pltpu.make_async_copy(wanted_v, wanted_s, loc_sem.at[3])
    w_load.start()
    p_load.wait()
    w_load.wait()

    in_tile = lax.broadcasted_iota(jnp.int32, (tile_rows, feature), 0)
    slots = send_buf.shape[1]

    def compute(b, k):
        for s in range(cap):
            chosen = wanted_s[b, s]
            tile = pas[chosen].astype(jnp.float32)
            tile = jnp.where(in_tile < len_ref[chosen], tile, tile[0:1, :])
            tiles[pl.ds(s * tile_rows, tile_rows), :] = tile.astype(tiles.dtype)
        total = None
        for u in range(*spans[k]):
            qs = qall[b, pl.ds(u * col, col), :]
            near = []
            for s in range(cap):
                sim = lax.dot_general(
                    tiles[pl.ds(s * tile_rows, tile_rows), :], qs,
                    (((1,), (1,)), ((), ())), preferred_element_type=jnp.float32)
                near.append(jnp.max(sim, axis=0, keepdims=True))
            if cap < slots:
                near.append(jnp.zeros((slots - cap, col), jnp.float32))
            near = jnp.concatenate(near, axis=0)
            high = near.astype(jnp.bfloat16).astype(jnp.float32)
            both = jnp.concatenate([high, near - high], axis=0).astype(jnp.bfloat16)
            part = jnp.dot(both, fold[pl.ds(u * col, col), :],
                           preferred_element_type=jnp.float32)
            part = part[:slots] + part[slots:]
            total = part if total is None else total + part
        total = total / float(tok)
        if k == 0:
            send_buf[b] = total
        else:
            send_buf[b] = send_buf[b] + total

    for k in range(2):
        share(0, 0, k, 1 - core).wait_recv()

    def near_body(j, _):
        b = at(pos, lax.rem(core + j, 2))
        for k in range(2):
            compute(b, k)

        @pl.when(j == 1)
        def _():
            score_copy(b).start()
        return 0

    lax.fori_loop(0, 2, near_body, 0)
    got[me] = send_buf[me]

    for s in range(1, half):
        for k in range(2):
            for d in range(2):
                hop_in(d, s, k).wait_recv()
                if has_hop(d, s + 1, k):
                    hop(d, s + 1, k).start()
                share(d, s, k, core).start()

            def ring_body(j, _, s=s, k=k):
                far = j // 2
                away = lax.rem(j, 2)
                step = (2 * away - 1) * s
                b = at(pos + step, lax.rem(core + far, 2))

                @pl.when(j == 2)
                def _():
                    for d in range(2):
                        share(d, s, k, 1 - core).wait_recv()
                compute(b, k)
                if k == 1:
                    score_copy(b).start()
                return 0

            lax.fori_loop(0, 4, ring_body, 0)
    for k in range(2):
        hop_in(k, half, k).wait_recv()
        share(k, half, k, core).start()

    def last_body(j, _):
        b = at(pos + half, lax.rem(core + j, 2))

        @pl.when(j == 1)
        def _():
            for k in range(2):
                share(k, half, k, 1 - core).wait_recv()
        for k in range(2):
            compute(b, k)
        score_copy(b).start()
        return 0

    lax.fori_loop(0, 2, last_body, 0)

    for k in range(2):
        share(0, 0, k, core).wait_send()
        for d in range(2):
            for s in range(1, half + 1):
                if has_hop(d, s, k):
                    hop(d, s, k).wait_send()
                    share(d, s, k, core).wait_send()
    each(1, lambda o: id_copy(o).wait_send())
    each(1, lambda o: score_copy(lax.rem(me + o, n)).wait_send())
    each(1, lambda o: score_in(o).wait_recv())
    out_ref[...] = got[...]


def local(ways, queries, passages, lengths, candidates):
    n = lax.axis_size("corpus")
    per_owner, tile_rows, feature = passages.shape
    per_device, tok = queries.shape[0], queries.shape[1]
    number = candidates.shape[1]
    rows = per_device * tok
    cap = max(2, 3 * number // (2 * n))
    slots = -(-cap // 8) * 8
    col = pick_tile(rows, tok)
    half = n // 4
    cfg = (n, ways, cap, per_owner, tile_rows, rows, feature, tok, col)
    got = pl.pallas_call(
        functools.partial(kernel, cfg),
        out_shape=jax.ShapeDtypeStruct((n, slots, 128), jnp.float32),
        in_specs=[
            pl.BlockSpec(memory_space=pltpu.VMEM),
            pl.BlockSpec(memory_space=pltpu.SMEM),
            pl.BlockSpec(memory_space=pl.ANY),
            pl.BlockSpec(memory_space=pl.ANY),
        ],
        out_specs=pl.BlockSpec(memory_space=pltpu.VMEM),
        scratch_shapes=[
            pltpu.VMEM((n, rows, feature), queries.dtype),
            pltpu.VMEM(passages.shape, passages.dtype),
            pltpu.VMEM((n, 1, number), jnp.int32),
            pltpu.VMEM((n, number), jnp.int32),
            pltpu.SMEM((n, number), jnp.int32),
            pltpu.VMEM((cap * tile_rows, feature), passages.dtype),
            pltpu.VMEM((rows, 128), jnp.bfloat16),
            pltpu.VMEM((n, slots, 128), jnp.float32),
            pltpu.VMEM((n, slots, 128), jnp.float32),
            pltpu.SemaphoreType.DMA((2, half + 1, 2)),
            pltpu.SemaphoreType.DMA((2, half + 1, 2)),
            pltpu.SemaphoreType.DMA((2, half + 1, 2)),
            pltpu.SemaphoreType.DMA((2, half + 1, 2)),
            pltpu.SemaphoreType.DMA((n,)),
            pltpu.SemaphoreType.DMA((n,)),
            pltpu.SemaphoreType.DMA((n,)),
            pltpu.SemaphoreType.DMA((n,)),
            pltpu.SemaphoreType.DMA((4,)),
        ],
        compiler_params=pltpu.CompilerParams(
            collective_id=0, has_side_effects=True, vmem_limit_bytes=60 * 2**20),
    )(candidates, lengths, queries.reshape(rows, feature), passages)

    ids = candidates[0]
    owner_of = ids // per_owner
    position = jnp.arange(number, dtype=jnp.int32)
    shared = (owner_of[:, None] == owner_of[None, :]) & (position[None, :] < position[:, None])
    slot_of = owner_of * slots + jnp.sum(shared.astype(jnp.int32), axis=1)
    picked = jnp.take(got.reshape(n * slots, 128), slot_of, axis=0)
    scores = picked.T[:per_device]
    best_scores = lax.top_k(scores, TOPK)[0]
    return (scores, best_scores)


def solution(mesh):
    ways = 2 if mesh.shape["groups"] == 2 else 1
    return jax.shard_map(
        functools.partial(local, ways),
        mesh=mesh,
        in_specs=(
            P(("groups", "corpus"), None, None),
            P(("groups", "corpus"), None, None),
            P(("groups", "corpus")),
            P(("groups", "corpus"), None),
        ),
        out_specs=(P(("groups", "corpus"), None), P(("groups", "corpus"), None)),
        check_vma=False,
    )
```

time: 137 us -> 72.2 us (0.53)
  Pallas kernels: 0 us -> 63.5 us
  waiting for transfers between devices: 49.2 us -> 0 us
  matrix products: 28.8 us -> 0 us
  local copies, waits for them, and re-layouts: 18.4 us -> 1.63 us
  between operations: 14.2 us -> 0.69 us
  starting transfers between devices: 10.9 us -> 0 us
  other arithmetic: 15.3 us -> 5.51 us
    pallas_call x0 -> x1, Pallas kernels: none -> 63.5 us  [local(): pl.pallas_call(functools.partial(kernel, cfg), out_shape=jax.ShapeDtypeSt...]
    all_gather x1 -> x0, waiting for transfers between devices: 36.8 us -> none  [local(): piece = lax.all_gather(stacked, 'corpus', axis=0, tiled=True)]
    dot_general x2 -> x0, matrix products: 28.8 us -> none  [maxsim_many(): jnp.einsum('srd,sgpd->srgp', query_sets, tile_sets, preferred_element_typ...]
    all_to_all x2 -> x0, waiting for transfers between devices: 11.7 us -> none  [the longest x1 6.72 us: local(): lax.all_to_all(fresh_scores, 'corpus', split_axis=0, concat_axis=0, tiled...]
    all_to_all x2 -> x0, starting transfers between devices: 10.9 us -> none  [the longest x1 7.41 us: local(): lax.all_to_all(wanted, 'corpus', split_axis=0, concat_axis=0, tiled=True)]
    gather x3 -> x1, local copies, waits for them, and re-layouts: 12.4 us -> 1.55 us  [local(): picked = jnp.take(got.reshape(n * slots, 128), slot_of, axis=0)]
    select_n x4 -> x3, other arithmetic: 7.96 us -> 1.49 us  [the longest x2 0.76 us: local(): picked = jnp.take(got.reshape(n * slots, 128), slot_of, axis=0)]
    reshape x4 -> x0, local copies, waits for them, and re-layouts: 1.66 us -> none  [the longest x2 1.61 us: maxsim_many(): nearest.reshape(shards_now, per_device, query_tok, nearest.shape[2])]
  transfers between devices with their start and end apart: 3 -> 0, of which waited for: 3 -> 0; matrix products, arithmetic and copies ran while one was open for 17% -> 0% of each run, Pallas kernels for 0% -> 0%
where the time goes in v1:
time: 72.2 us; the launch traced here: 71.3 us
  Pallas kernels  63.5 us (88%)
  other arithmetic  5.51 us (8%)
  local copies, waits for them, and re-layouts  1.63 us (2%)
    pallas_call x1, Pallas kernels, local(): pl.pallas_call(functools.partial(kernel, cfg), out_shape=jax.ShapeDtypeSt...  63.5 us
    top_k x1, other arithmetic, local(): best_scores = lax.top_k(scores, TOPK)[0]  3.17 us
    gather x1, local copies, waits for them, and re-layouts, local(): picked = jnp.take(got.reshape(n * slots, 128), slot_of, axis=0)  1.55 us

profile of v1, /device:TPU:0, one launch (start us, length us, event | category | flops | bytes accessed | tf_op | source)
XLA Modules:
  0.0 71.3 jit_solution(5669394279015023119)
XLA Ops:
  0.6 0.0 copy-start.1
  0.6 0.7 %and_select_fusion.2 = s32[128]{0:T(128)S(1)} fusion(s32[1,128]{1,0:T(1,128)} %cand_ref.1), kind=kLoop, calls=%fused_computation.11 | loop fusion | flops 1920 | bytes 1024 | tf_op jit(solution)/shard_map/jit(floor_divide)/jit(_where)/select_n | solution.py:317
  1.4 0.7 fusion.2
  2.0 0.2 convert_reduce_fusion
  2.2 0.7 fusion.1
  2.9 63.5 %shard_map.59 = f32[16,16,128]{2,1,0:T(8,128)} custom-call(s32[1,128]{1,0:T(1,128)} %cand_ref.1, s32[128]{0:T(128)} %len_ref.1, bf16[1792,128]{1,0:T(8,128)(2,1)} %bitcast.35, bf16[128,128,128]{2,1,0:T(8,128)(2,1)} %p_hbm.1), custom_call_target="tpu_custom_call" | custom-call | tf_op jit(solution)/shard_map/pallas_call | solution.py:282
  66.4 1.5 %gather_fusion = f32[128,128]{1,0:T(8,128)S(1)} fusion(f32[256,128]{1,0:T(8,128)} %bitcast.34, s32[1024]{0:T(1024)S(1)} %pad_clamp_fusion), kind=kCustom, calls=%fused_computation | custom fusion | bytes 131584 | tf_op jit(solution)/shard_map/jit(_take)/gather | solution.py:321
  67.9 0.0 copy-done.1
  68.0 0.1 select_bitcast_fusion
  68.0 0.1 copy.10
  68.1 0.0 copy-start
  68.1 3.2 %top_k.9 = (f32[56,128]{1,0:T(8,128)}, s32[56,128]{1,0:T(8,128)}) sort(f32[56,128]{1,0:T(8,128)S(1)} %copy.10, s32[56,128]{1,0:T(8,128)S(1)} %iota.10), dimensions={1}, to_apply=%region_1.2 | sort | flops 93184 | bytes 114688 | tf_op jit(solution)/shard_map/top_k | solution.py:323
  71.3 0.0 copy-done
  (3 shorter events, 0.0 us)
Async XLA Ops:
  0.6 67.3 %copy-start.1 = (s32[1,128]{1,0:T(1,128)S(1)}, s32[1,128]{1,0:T(1,128)}, u32[]{:S(2)}) copy-start(s32[1,128]{1,0:T(1,128)} %cand_ref.1) | copy-start | bytes 1540
  68.1 3.2 %copy-start = (f32[56,128]{1,0:T(8,128)}, f32[56,128]{1,0:T(8,128)S(1)}, u32[]{:S(2)}) copy-start(f32[56,128]{1,0:T(8,128)S(1)} %copy.10) | copy-start | bytes 86020

commit v2 on v1

--- a/solution.py
+++ b/solution.py
@@ -18,8 +18,40 @@
     return tile
 
 
-def kernel(cfg, cand_ref, len_ref, q_hbm, p_hbm, out_ref, qall, pas, cand_all,
-           wanted_v, wanted_s, tiles, fold, send_buf, got, q_send, q_recv,
+def sort_down(x):
+    count, width = x.shape
+    index = lax.broadcasted_iota(jnp.int32, (count // 8, 8, width), 0) * 8
+    index = index + lax.broadcasted_iota(jnp.int32, (count // 8, 8, width), 1)
+    x = x.reshape(count // 8, 8, width)
+    size = 2
+    while size <= count:
+        gap = size // 2
+        falling = (index // size) % 2 == 0
+        while gap >= 1:
+            low = (index // gap) % 2 == 0
+            if gap >= 8:
+                hop = gap // 8
+                y = x.reshape(count // (2 * gap), 2, hop, 8, width)
+                y = jnp.concatenate([y[:, 1:], y[:, :1]], axis=1)
+                other = y.reshape(x.shape)
+            else:
+                other = jnp.where(low, pltpu.roll(x, 8 - gap, 1), pltpu.roll(x, gap, 1))
+            x = jnp.where(low == falling, jnp.maximum(x, other), jnp.minimum(x, other))
+            gap //= 2
+        size *= 2
+    return x.reshape(count, width)
+
+
+def split3(x):
+    high = x.astype(jnp.bfloat16)
+    rest = x - high.astype(jnp.float32)
+    mid = rest.astype(jnp.bfloat16)
+    low = (rest - mid.astype(jnp.float32)).astype(jnp.bfloat16)
+    return high, mid, low
+
+
+def kernel(cfg, cand_ref, len_ref, q_hbm, p_hbm, out_ref, best_ref, qall, pas, cand_all,
+           wanted_v, wanted_s, place, fold, send_buf, got, q_send, q_recv,
            sib_send, sib_recv, id_send, id_recv, sc_send, sc_recv, loc_sem):
     n, ways, cap, per_owner, tile_rows, rows, feature, tok, col = cfg
     chips = n // 2
@@ -124,6 +156,17 @@
     row_at = lax.broadcasted_iota(jnp.int32, (rows, 128), 0) // tok
     lane_at = lax.broadcasted_iota(jnp.int32, (rows, 128), 1)
     fold[...] = jnp.where(row_at == lane_at, 1.0, 0.0).astype(fold.dtype)
+    slots = send_buf.shape[1]
+    number = cand_ref.shape[1]
+    mine_row = lax.div(cand_ref[...], per_owner).astype(jnp.float32)
+    across = jnp.broadcast_to(mine_row, (number, number))
+    down = across.T
+    r_at = lax.broadcasted_iota(jnp.int32, (number, number), 0)
+    c_at = lax.broadcasted_iota(jnp.int32, (number, number), 1)
+    ahead = jnp.where((across == down) & (c_at < r_at), 1.0, 0.0)
+    slot = down[:, :1] * float(slots) + jnp.sum(ahead, axis=1, keepdims=True)
+    slot_at = lax.broadcasted_iota(jnp.int32, place.shape, 1).astype(jnp.float32)
+    place[...] = jnp.where(slot_at == slot, 1.0, 0.0).astype(place.dtype)
     c_load.wait()
     q_load.wait()
     pl.semaphore_wait(barrier, n - 1)
@@ -140,15 +183,24 @@
             if has_hop(d, 1, k):
                 hop(d, 1, k).start()
         share(0, 0, k, core).start()
+    in_tile = lax.broadcasted_iota(jnp.int32, (tile_rows, feature), 0)
+    p_load.wait()
+
+    def fill(i, _):
+        for j in range(4):
+            p = i * 4 + j
+            tile = pas[p].astype(jnp.float32)
+            tile = jnp.where(in_tile < len_ref[p], tile, tile[0:1, :])
+            pas[p] = tile.astype(pas.dtype)
+        return 0
+
+    lax.fori_loop(0, per_owner // 4, fill, 0)
     each(1, lambda o: id_in(o).wait_recv())
 
     ids = cand_all[...].reshape(n, cand_all.shape[2])
-    number = ids.shape[1]
     owner = lax.div(ids, per_owner)
     local = ids - owner * per_owner
     mine = owner == me
-    r_at = lax.broadcasted_iota(jnp.int32, (number, number), 0)
-    c_at = lax.broadcasted_iota(jnp.int32, (number, number), 1)
     before = jnp.where(r_at < c_at, 1.0, 0.0).astype(jnp.bfloat16)
     rank = jnp.dot(jnp.where(mine, 1.0, 0.0).astype(jnp.bfloat16), before,
                    preferred_element_type=jnp.float32)
@@ -161,49 +213,34 @@
     wanted_v[...] = wanted
     w_load = pltpu.make_async_copy(wanted_v, wanted_s, loc_sem.at[3])
     w_load.start()
-    p_load.wait()
     w_load.wait()
 
-    in_tile = lax.broadcasted_iota(jnp.int32, (tile_rows, feature), 0)
-    slots = send_buf.shape[1]
-
     def compute(b, k):
-        for s in range(cap):
-            chosen = wanted_s[b, s]
-            tile = pas[chosen].astype(jnp.float32)
-            tile = jnp.where(in_tile < len_ref[chosen], tile, tile[0:1, :])
-            tiles[pl.ds(s * tile_rows, tile_rows), :] = tile.astype(tiles.dtype)
-        total = None
+        chosen = [wanted_s[b, s] for s in range(cap)]
+        pieces = []
         for u in range(*spans[k]):
             qs = qall[b, pl.ds(u * col, col), :]
             near = []
             for s in range(cap):
-                sim = lax.dot_general(
-                    tiles[pl.ds(s * tile_rows, tile_rows), :], qs,
-                    (((1,), (1,)), ((), ())), preferred_element_type=jnp.float32)
+                sim = lax.dot_general(pas[chosen[s]], qs, (((1,), (1,)), ((), ())),
+                                      preferred_element_type=jnp.float32)
                 near.append(jnp.max(sim, axis=0, keepdims=True))
             if cap < slots:
                 near.append(jnp.zeros((slots - cap, col), jnp.float32))
             near = jnp.concatenate(near, axis=0)
             high = near.astype(jnp.bfloat16).astype(jnp.float32)
-            both = jnp.concatenate([high, near - high], axis=0).astype(jnp.bfloat16)
-            part = jnp.dot(both, fold[pl.ds(u * col, col), :],
-                           preferred_element_type=jnp.float32)
-            part = part[:slots] + part[slots:]
-            total = part if total is None else total + part
-        total = total / float(tok)
-        if k == 0:
-            send_buf[b] = total
-        else:
-            send_buf[b] = send_buf[b] + total
+            pieces.append(jnp.concatenate([high, near - high], axis=0).astype(jnp.bfloat16))
+        lo, hi = spans[k]
+        part = jnp.dot(jnp.concatenate(pieces, axis=1), fold[pl.ds(lo * col, (hi - lo) * col), :],
+                       preferred_element_type=jnp.float32)
+        return (part[:slots] + part[slots:]) / float(tok)
 
     for k in range(2):
         share(0, 0, k, 1 - core).wait_recv()
 
     def near_body(j, _):
         b = at(pos, lax.rem(core + j, 2))
-        for k in range(2):
-            compute(b, k)
+        send_buf[b] = compute(b, 0) + compute(b, 1)
 
         @pl.when(j == 1)
         def _():
@@ -222,21 +259,20 @@
                 share(d, s, k, core).start()
 
             def ring_body(j, _, s=s, k=k):
-                far = j // 2
-                away = lax.rem(j, 2)
-                step = (2 * away - 1) * s
-                b = at(pos + step, lax.rem(core + far, 2))
-
-                @pl.when(j == 2)
+                @pl.when(j == 1)
                 def _():
                     for d in range(2):
                         share(d, s, k, 1 - core).wait_recv()
-                compute(b, k)
+                blocks = [origin(d, s, lax.rem(core + j, 2)) for d in range(2)]
+                found = [compute(b, k) for b in blocks]
+                for b, part in zip(blocks, found):
+                    send_buf[b] = part if k == 0 else send_buf[b] + part
                 if k == 1:
-                    score_copy(b).start()
+                    for b in blocks:
+                        score_copy(b).start()
                 return 0
 
-            lax.fori_loop(0, 4, ring_body, 0)
+            lax.fori_loop(0, 2, ring_body, 0)
     for k in range(2):
         hop_in(k, half, k).wait_recv()
         share(k, half, k, core).start()
@@ -248,8 +284,7 @@
         def _():
             for k in range(2):
                 share(k, half, k, 1 - core).wait_recv()
-        for k in range(2):
-            compute(b, k)
+        send_buf[b] = compute(b, 0) + compute(b, 1)
         score_copy(b).start()
         return 0
 
@@ -265,7 +300,14 @@
     each(1, lambda o: id_copy(o).wait_send())
     each(1, lambda o: score_copy(lax.rem(me + o, n)).wait_send())
     each(1, lambda o: score_in(o).wait_recv())
-    out_ref[...] = got[...]
+    flat = got[...].reshape(n * slots, got.shape[2])
+    spread = None
+    for part in split3(flat):
+        term = jnp.dot(place[...], part, preferred_element_type=jnp.float32)
+        spread = term if spread is None else spread + term
+    queries = out_ref.shape[0]
+    out_ref[...] = spread.T[:queries]
+    best_ref[...] = sort_down(spread).T[:queries, :best_ref.shape[1]]
 
 
 def local(ways, queries, passages, lengths, candidates):
@@ -279,23 +321,29 @@
     col = pick_tile(rows, tok)
     half = n // 4
     cfg = (n, ways, cap, per_owner, tile_rows, rows, feature, tok, col)
-    got = pl.pallas_call(
+    return pl.pallas_call(
         functools.partial(kernel, cfg),
-        out_shape=jax.ShapeDtypeStruct((n, slots, 128), jnp.float32),
+        out_shape=(
+            jax.ShapeDtypeStruct((per_device, number), jnp.float32),
+            jax.ShapeDtypeStruct((per_device, TOPK), jnp.float32),
+        ),
         in_specs=[
             pl.BlockSpec(memory_space=pltpu.VMEM),
             pl.BlockSpec(memory_space=pltpu.SMEM),
             pl.BlockSpec(memory_space=pl.ANY),
             pl.BlockSpec(memory_space=pl.ANY),
         ],
-        out_specs=pl.BlockSpec(memory_space=pltpu.VMEM),
+        out_specs=(
+            pl.BlockSpec(memory_space=pltpu.VMEM),
+            pl.BlockSpec(memory_space=pltpu.VMEM),
+        ),
         scratch_shapes=[
             pltpu.VMEM((n, rows, feature), queries.dtype),
             pltpu.VMEM(passages.shape, passages.dtype),
             pltpu.VMEM((n, 1, number), jnp.int32),
             pltpu.VMEM((n, number), jnp.int32),
             pltpu.SMEM((n, number), jnp.int32),
-            pltpu.VMEM((cap * tile_rows, feature), passages.dtype),
+            pltpu.VMEM((number, n * slots), jnp.bfloat16),
             pltpu.VMEM((rows, 128), jnp.bfloat16),
             pltpu.VMEM((n, slots, 128), jnp.float32),
             pltpu.VMEM((n, slots, 128), jnp.float32),
@@ -313,16 +361,6 @@
             collective_id=0, has_side_effects=True, vmem_limit_bytes=60 * 2**20),
     )(candidates, lengths, queries.reshape(rows, feature), passages)
 
-    ids = candidates[0]
-    owner_of = ids // per_owner
-    position = jnp.arange(number, dtype=jnp.int32)
-    shared = (owner_of[:, None] == owner_of[None, :]) & (position[None, :] < position[:, None])
-    slot_of = owner_of * slots + jnp.sum(shared.astype(jnp.int32), axis=1)
-    picked = jnp.take(got.reshape(n * slots, 128), slot_of, axis=0)
-    scores = picked.T[:per_device]
-    best_scores = lax.top_k(scores, TOPK)[0]
-    return (scores, best_scores)
-
 
 def solution(mesh):
     ways = 2 if mesh.shape["groups"] == 2 else 1

time: 72.2 us -> 57.6 us (0.80)
  Pallas kernels: 63.5 us -> 53.5 us
  other arithmetic: 5.51 us -> 0 us
  local copies, waits for them, and re-layouts: 1.63 us -> 2.72 us
    pallas_call x1, Pallas kernels: 63.5 us -> 53.5 us  [local(): pl.pallas_call(functools.partial(kernel, cfg), out_shape=(jax.ShapeDtypeS...]
    top_k x1 -> x0, other arithmetic: 3.17 us -> none  [local(): best_scores = lax.top_k(scores, TOPK)[0]]
    unnamed x5 -> x2, local copies, waits for them, and re-layouts: 0.07 us -> 2.72 us
    gather x1 -> x0, local copies, waits for them, and re-layouts: 1.55 us -> none  [local(): picked = jnp.take(got.reshape(n * slots, 128), slot_of, axis=0)]
    select_n x3 -> x0, other arithmetic: 1.49 us -> none  [the longest x2 0.76 us: local(): picked = jnp.take(got.reshape(n * slots, 128), slot_of, axis=0)]
where the time goes in v2:
time: 57.6 us; the launch traced here: 56.8 us
  Pallas kernels  53.5 us (93%)
  local copies, waits for them, and re-layouts  2.72 us (5%)
  between operations  0.64 us (1%)
    pallas_call x1, Pallas kernels, local(): pl.pallas_call(functools.partial(kernel, cfg), out_shape=(jax.ShapeDtypeS...  53.5 us
    unnamed x2, local copies, waits for them, and re-layouts  2.72 us

profile of v2, /device:TPU:0, one launch (start us, length us, event | category | flops | bytes accessed | tf_op | source)
XLA Modules:
  0.0 56.8 jit_solution(12003164272482820949)
XLA Ops:
  0.6 53.5 %shard_map.59 = (f32[56,128]{1,0:T(8,128)}, f32[56,100]{1,0:T(8,128)}) custom-call(s32[1,128]{1,0:T(1,128)} %cand_ref.1, s32[128]{0:T(128)} %len_ref.1, bf16[1792,128]{1,0:T(8,128)(2,1)} %bitcast.1, bf16[128,128,128]{2,1,0:T(8,128)(2,1)} %p_hbm.1), custom_call_target="tpu_custom_call" | custom-call | tf_op jit(solution)/shard_map/pallas_call | solution.py:324
  54.1 1.4 %copy.8 = f32[56,128]{1,0:T(8,128)} copy(f32[56,128]{1,0:T(8,128)} %get-tuple-element.4) | data formatting | bytes 57344
  55.4 1.4 %copy.9 = f32[56,100]{1,0:T(8,128)} copy(f32[56,100]{1,0:T(8,128)} %get-tuple-element.5) | data formatting | bytes 44800

commit v3 on v2

--- a/solution.py
+++ b/solution.py
@@ -50,7 +50,7 @@
     return high, mid, low
 
 
-def kernel(cfg, cand_ref, len_ref, q_hbm, p_hbm, out_ref, best_ref, qall, pas, cand_all,
+def kernel(cfg, cand_ref, len_ref, q_hbm, p_hbm, out_ref, place_ref, qall, pas, cand_all,
            wanted_v, wanted_s, place, fold, send_buf, got, q_send, q_recv,
            sib_send, sib_recv, id_send, id_recv, sc_send, sc_recv, loc_sem):
     n, ways, cap, per_owner, tile_rows, rows, feature, tok, col = cfg
@@ -60,6 +60,7 @@
     units = rows // col
     cut = (units + 1) // 2
     spans = ((0, cut), (cut, units))
+    ends = tuple(((lo, (lo + hi + 1) // 2), ((lo + hi + 1) // 2, hi)) for lo, hi in spans)
     me = lax.axis_index("corpus")
     core = lax.rem(me, 2)
     chip = me // 2
@@ -83,33 +84,30 @@
     def origin(d, s, c):
         return at(pos - s if d == 0 else pos + s, c)
 
-    def piece(b, k):
-        lo, hi = spans[k]
+    def piece(b, d, s, k):
+        lo, hi = ends[d][k] if s == half else spans[k]
         return qall.at[b, pl.ds(lo * col, (hi - lo) * col), :]
 
     def hop(d, s, k):
         b = origin(d, s - 1, core)
         return pltpu.make_async_remote_copy(
-            src_ref=piece(b, k), dst_ref=piece(b, k),
+            src_ref=piece(b, d, s, k), dst_ref=piece(b, d, s, k),
             send_sem=q_send.at[d, s, k], recv_sem=q_recv.at[d, s, k],
             device_id={"corpus": toward[d]}, device_id_type=MESH)
 
     def hop_in(d, s, k):
         b = origin(d, s, core)
         return pltpu.make_async_remote_copy(
-            src_ref=piece(b, k), dst_ref=piece(b, k),
+            src_ref=piece(b, d, s, k), dst_ref=piece(b, d, s, k),
             send_sem=q_send.at[d, s, k], recv_sem=q_recv.at[d, s, k],
             device_id={"corpus": toward[d]}, device_id_type=MESH)
 
     def share(d, s, k, c):
         b = origin(d, s, c)
         return pltpu.make_async_remote_copy(
-            src_ref=piece(b, k), dst_ref=piece(b, k),
+            src_ref=piece(b, d, s, k), dst_ref=piece(b, d, s, k),
             send_sem=sib_send.at[d, s, k], recv_sem=sib_recv.at[d, s, k],
             device_id={"corpus": sib}, device_id_type=MESH)
-
-    def has_hop(d, s, k):
-        return 1 <= s < half or (s == half and k == d)
 
     def id_copy(o):
         peer = lax.rem(me + o, n)
@@ -180,8 +178,7 @@
     each(1, lambda o: id_copy(o).start())
     for k in range(2):
         for d in range(2):
-            if has_hop(d, 1, k):
-                hop(d, 1, k).start()
+            hop(d, 1, k).start()
         share(0, 0, k, core).start()
     in_tile = lax.broadcasted_iota(jnp.int32, (tile_rows, feature), 0)
     p_load.wait()
@@ -215,10 +212,10 @@
     w_load.start()
     w_load.wait()
 
-    def compute(b, k):
+    def compute(b, lo, hi):
         chosen = [wanted_s[b, s] for s in range(cap)]
         pieces = []
-        for u in range(*spans[k]):
+        for u in range(lo, hi):
             qs = qall[b, pl.ds(u * col, col), :]
             near = []
             for s in range(cap):
@@ -230,7 +227,6 @@
             near = jnp.concatenate(near, axis=0)
             high = near.astype(jnp.bfloat16).astype(jnp.float32)
             pieces.append(jnp.concatenate([high, near - high], axis=0).astype(jnp.bfloat16))
-        lo, hi = spans[k]
         part = jnp.dot(jnp.concatenate(pieces, axis=1), fold[pl.ds(lo * col, (hi - lo) * col), :],
                        preferred_element_type=jnp.float32)
         return (part[:slots] + part[slots:]) / float(tok)
@@ -240,7 +236,7 @@
 
     def near_body(j, _):
         b = at(pos, lax.rem(core + j, 2))
-        send_buf[b] = compute(b, 0) + compute(b, 1)
+        send_buf[b] = compute(b, *spans[0]) + compute(b, *spans[1])
 
         @pl.when(j == 1)
         def _():
@@ -254,8 +250,11 @@
         for k in range(2):
             for d in range(2):
                 hop_in(d, s, k).wait_recv()
-                if has_hop(d, s + 1, k):
+                if s + 1 < half:
                     hop(d, s + 1, k).start()
+                elif k == d:
+                    for m in range(2):
+                        hop(d, half, m).start()
                 share(d, s, k, core).start()
 
             def ring_body(j, _, s=s, k=k):
@@ -264,7 +263,7 @@
                     for d in range(2):
                         share(d, s, k, 1 - core).wait_recv()
                 blocks = [origin(d, s, lax.rem(core + j, 2)) for d in range(2)]
-                found = [compute(b, k) for b in blocks]
+                found = [compute(b, *spans[k]) for b in blocks]
                 for b, part in zip(blocks, found):
                     send_buf[b] = part if k == 0 else send_buf[b] + part
                 if k == 1:
@@ -273,37 +272,43 @@
                 return 0
 
             lax.fori_loop(0, 2, ring_body, 0)
-    for k in range(2):
-        hop_in(k, half, k).wait_recv()
-        share(k, half, k, core).start()
-
-    def last_body(j, _):
-        b = at(pos + half, lax.rem(core + j, 2))
-
-        @pl.when(j == 1)
-        def _():
-            for k in range(2):
-                share(k, half, k, 1 - core).wait_recv()
-        send_buf[b] = compute(b, 0) + compute(b, 1)
-        score_copy(b).start()
-        return 0
-
-    lax.fori_loop(0, 2, last_body, 0)
+    for m in range(2):
+        for d in range(2):
+            hop_in(d, half, m).wait_recv()
+            share(d, half, m, core).start()
+
+        def last_body(j, _, m=m):
+            b = at(pos + half, lax.rem(core + j, 2))
+
+            @pl.when(j == 1)
+            def _():
+                for d in range(2):
+                    share(d, half, m, 1 - core).wait_recv()
+            part = compute(b, *ends[0][m]) + compute(b, *ends[1][m])
+            send_buf[b] = part if m == 0 else send_buf[b] + part
+            if m == 1:
+                score_copy(b).start()
+            return 0
+
+        lax.fori_loop(0, 2, last_body, 0)
 
     for k in range(2):
         share(0, 0, k, core).wait_send()
         for d in range(2):
             for s in range(1, half + 1):
-                if has_hop(d, s, k):
-                    hop(d, s, k).wait_send()
-                    share(d, s, k, core).wait_send()
+                hop(d, s, k).wait_send()
+                share(d, s, k, core).wait_send()
     each(1, lambda o: id_copy(o).wait_send())
     each(1, lambda o: score_copy(lax.rem(me + o, n)).wait_send())
     each(1, lambda o: score_in(o).wait_recv())
-    flat = got[...].reshape(n * slots, got.shape[2])
+    out_ref[...] = got[...].reshape(out_ref.shape)
+    place_ref[...] = place[...]
+
+
+def finish(got_ref, place_ref, out_ref, best_ref):
     spread = None
-    for part in split3(flat):
-        term = jnp.dot(place[...], part, preferred_element_type=jnp.float32)
+    for part in split3(got_ref[...]):
+        term = jnp.dot(place_ref[...], part, preferred_element_type=jnp.float32)
         spread = term if spread is None else spread + term
     queries = out_ref.shape[0]
     out_ref[...] = spread.T[:queries]
@@ -321,11 +326,11 @@
     col = pick_tile(rows, tok)
     half = n // 4
     cfg = (n, ways, cap, per_owner, tile_rows, rows, feature, tok, col)
-    return pl.pallas_call(
+    got, place = pl.pallas_call(
         functools.partial(kernel, cfg),
         out_shape=(
-            jax.ShapeDtypeStruct((per_device, number), jnp.float32),
-            jax.ShapeDtypeStruct((per_device, TOPK), jnp.float32),
+            jax.ShapeDtypeStruct((n * slots, 128), jnp.float32),
+            jax.ShapeDtypeStruct((number, n * slots), jnp.bfloat16),
         ),
         in_specs=[
             pl.BlockSpec(memory_space=pltpu.VMEM),
@@ -360,6 +365,15 @@
         compiler_params=pltpu.CompilerParams(
             collective_id=0, has_side_effects=True, vmem_limit_bytes=60 * 2**20),
     )(candidates, lengths, queries.reshape(rows, feature), passages)
+    return pl.pallas_call(
+        finish,
+        out_shape=(
+            jax.ShapeDtypeStruct((per_device, number), jnp.float32),
+            jax.ShapeDtypeStruct((per_device, TOPK), jnp.float32),
+        ),
+        in_specs=[pl.BlockSpec(memory_space=pltpu.VMEM)] * 2,
+        out_specs=(pl.BlockSpec(memory_space=pltpu.VMEM), pl.BlockSpec(memory_space=pltpu.VMEM)),
+    )(got, place)
 
 
 def solution(mesh):

time: 57.6 us -> 56.8 us (0.986); the launches traced: 56.8 us -> 56.7 us
  local copies, waits for them, and re-layouts: 2.72 us -> 0 us
  Pallas kernels: 53.5 us -> 56 us
    unnamed x2 -> x0, local copies, waits for them, and re-layouts: 2.72 us -> none
    pallas_call x0 -> x1, Pallas kernels: none -> 2.08 us  [local(): pl.pallas_call(finish, out_shape=(jax.ShapeDtypeStruct((per_device, numbe...]
where the time goes in v3:
time: 56.8 us; the launch traced here: 56.7 us
  Pallas kernels  56 us (99%)
  between operations  0.64 us (1%)
    pallas_call x1, Pallas kernels, local(): pl.pallas_call(functools.partial(kernel, cfg), out_shape=(jax.ShapeDtypeS...  53.9 us
    pallas_call x1, Pallas kernels, local(): pl.pallas_call(finish, out_shape=(jax.ShapeDtypeStruct((per_device, numbe...  2.08 us

profile of v3, /device:TPU:0, one launch (start us, length us, event | category | flops | bytes accessed | tf_op | source)
XLA Modules:
  0.0 56.7 jit_solution(3423838546124533217)
XLA Ops:
  0.6 53.9 %shard_map.59 = (f32[256,128]{1,0:T(8,128)}, bf16[128,256]{1,0:T(8,128)(2,1)}) custom-call(s32[1,128]{1,0:T(1,128)} %cand_ref.1, s32[128]{0:T(128)} %len_ref.1, bf16[1792,128]{1,0:T(8,128)(2,1)} %bitcast.1, bf16[128,128,128]{2,1,0:T(8,128)(2,1)} %p_hbm.1), custom_call_target="tpu_custom_call" | custom-call | tf_op jit(solution)/shard_map/pallas_call | solution.py:329
  54.6 2.1 %shard_map.60 = (f32[56,128]{1,0:T(8,128)}, f32[56,100]{1,0:T(8,128)}) custom-call(f32[256,128]{1,0:T(8,128)} %get-tuple-element.4.got_ref, bf16[128,256]{1,0:T(8,128)(2,1)} %get-tuple-element.5.place_ref), custom_call_target="tpu_custom_call" | custom-call | tf_op jit(solution)/shard_map/pallas_call | solution.py:368

commit v4 on v3

--- a/solution.py
+++ b/solution.py
@@ -151,6 +151,21 @@
         return 0
 
     lax.fori_loop(1, n, greet, 0)
+    c_load.wait()
+    q_load.wait()
+    pl.semaphore_wait(barrier, n - 1)
+
+    def each(first, fn):
+        def body(o, _):
+            fn(o)
+            return 0
+        lax.fori_loop(first, n, body, 0)
+
+    each(1, lambda o: id_copy(o).start())
+    for k in range(2):
+        for d in range(2):
+            hop(d, 1, k).start()
+        share(0, 0, k, core).start()
     row_at = lax.broadcasted_iota(jnp.int32, (rows, 128), 0) // tok
     lane_at = lax.broadcasted_iota(jnp.int32, (rows, 128), 1)
     fold[...] = jnp.where(row_at == lane_at, 1.0, 0.0).astype(fold.dtype)
@@ -165,21 +180,6 @@
     slot = down[:, :1] * float(slots) + jnp.sum(ahead, axis=1, keepdims=True)
     slot_at = lax.broadcasted_iota(jnp.int32, place.shape, 1).astype(jnp.float32)
     place[...] = jnp.where(slot_at == slot, 1.0, 0.0).astype(place.dtype)
-    c_load.wait()
-    q_load.wait()
-    pl.semaphore_wait(barrier, n - 1)
-
-    def each(first, fn):
-        def body(o, _):
-            fn(o)
-            return 0
-        lax.fori_loop(first, n, body, 0)
-
-    each(1, lambda o: id_copy(o).start())
-    for k in range(2):
-        for d in range(2):
-            hop(d, 1, k).start()
-        share(0, 0, k, core).start()
     in_tile = lax.broadcasted_iota(jnp.int32, (tile_rows, feature), 0)
     p_load.wait()
 

time: 56.8 us -> 56.8 us (level)
  no operation moved by 1% of the time
where the time goes in v4:
time: 56.8 us; the launch traced here: 56.7 us
  Pallas kernels  56 us (99%)
  between operations  0.64 us (1%)
    pallas_call x1, Pallas kernels, local(): pl.pallas_call(functools.partial(kernel, cfg), out_shape=(jax.ShapeDtypeS...  53.9 us
    pallas_call x1, Pallas kernels, local(): pl.pallas_call(finish, out_shape=(jax.ShapeDtypeStruct((per_device, numbe...  2.08 us

profile of v4, /device:TPU:0, one launch (start us, length us, event | category | flops | bytes accessed | tf_op | source)
XLA Modules:
  0.0 56.7 jit_solution(8194697814783191232)
XLA Ops:
  0.6 53.9 %shard_map.59 = (f32[256,128]{1,0:T(8,128)}, bf16[128,256]{1,0:T(8,128)(2,1)}) custom-call(s32[1,128]{1,0:T(1,128)} %cand_ref.1, s32[128]{0:T(128)} %len_ref.1, bf16[1792,128]{1,0:T(8,128)(2,1)} %bitcast.1, bf16[128,128,128]{2,1,0:T(8,128)(2,1)} %p_hbm.1), custom_call_target="tpu_custom_call" | custom-call | tf_op jit(solution)/shard_map/pallas_call | solution.py:329
  54.6 2.1 %shard_map.60 = (f32[56,128]{1,0:T(8,128)}, f32[56,100]{1,0:T(8,128)}) custom-call(f32[256,128]{1,0:T(8,128)} %get-tuple-element.4.got_ref, bf16[128,256]{1,0:T(8,128)(2,1)} %get-tuple-element.5.place_ref), custom_call_target="tpu_custom_call" | custom-call | tf_op jit(solution)/shard_map/pallas_call | solution.py:368
